TPU v7x, 32 devices: a whole 2x2x4 slice. The times are simulated.
32 devices in a mesh: row: 4 (over x, core), col: 8 (over z, y).
Axes of the slice: x: 2, y: 2, z: 4, core: 2. Of those that a mesh axis runs over, the one named last changes fastest.
Arguments:
- schur: float32 [4096, 4096], P('row', 'col'), may hold values from -6 to 6
- left_rot: float32 [8, 512, 512], P('row', 'col'), may hold values from -1 to 1, as said below
- right_rot: float32 [8, 512, 512], P('col', 'row'), may hold values from -1 to 1, as said below
- left_off: float32 [8, 512, 512], P('row', 'col'), may hold values from -1 to 1, as said below
- right_off: float32 [8, 512, 512], P('col', 'row'), may hold values from -1 to 1, as said below
Outputs:
- updated: float32 [4096, 4096], P('row', 'col')
Inputs may be any that keep to these rules, and one draw needn't show every extreme that they name: `left_rot`: each 512 x 512 block is orthogonal. `right_rot`: each 512 x 512 block is orthogonal. `left_off`: each 512 x 512 block is orthogonal. `right_off`: each 512 x 512 block is orthogonal.
All inputs are finite; a program needn't handle non-finite values.
Results may differ from a plain program's by a relative error of at most 0.00007.
Values sent between devices are 32-bit elements; how exact they have to be, the bound alone decides.
A program may use at most 64 MiB of HBM per device.

v0:
```python
import jax
import jax.numpy as jnp
from jax import lax
from jax.sharding import PartitionSpec as P


def passed_along(x, axis, by):
    size = lax.axis_size(axis)
    return lax.ppermute(x, axis, [(i, (i + by) % size) for i in range(size)])


def padded_2(cells, sides, width):
    for axis, dim in sides:
        count = lax.axis_size(axis)
        head = lax.slice_in_dim(cells, 0, width, axis=dim)
        tail = lax.slice_in_dim(cells, cells.shape[dim] - width, cells.shape[dim], axis=dim)
        cells = jnp.concatenate(
            [
                lax.ppermute(tail, axis, [(i, (i + 1) % count) for i in range(count)]),
                cells,
                lax.ppermute(head, axis, [((i + 1) % count, i) for i in range(count)]),
            ],
            axis=dim,
        )
    return cells


def apply_left(blocks, rotations):
    number = rotations.shape[0]
    window = rotations.shape[1]
    shaped = blocks.reshape(number, window, blocks.shape[1])
    result = jnp.einsum("kab,kac->kbc", rotations, shaped, precision=lax.Precision.HIGHEST)
    return result.reshape(number * window, blocks.shape[1])


def apply_right(blocks, rotations):
    number = rotations.shape[0]
    window = rotations.shape[1]
    shaped = blocks.reshape(blocks.shape[0], number, window)
    result = jnp.einsum("rka,kab->rkb", shaped, rotations, precision=lax.Precision.HIGHEST)
    return result.reshape(blocks.shape[0], number * window)


def body(schur, left_rot, right_rot, left_off, right_off):
    window = left_rot.shape[2]
    half_window = window // 2
    rows_here = schur.shape[0]
    cols_here = schur.shape[1]
    rotations = lax.all_gather(right_rot, "row", axis=1, tiled=True)
    matrix = apply_right(schur, rotations)
    rotations = lax.all_gather(left_rot, "col", axis=1, tiled=True)
    matrix = apply_left(matrix, rotations)
    rotations = lax.all_gather(right_off, "row", axis=1, tiled=True)
    following = passed_along(rotations[0][:, :half_window], "col", -1)
    padded = padded_2(matrix, (("col", 1),), half_window)
    leading = jnp.dot(
        padded[:, :window], rotations[0][:, half_window:], precision=lax.Precision.HIGHEST
    )
    middle = apply_right(padded[:, window:cols_here], rotations[1:])
    trailing = jnp.dot(
        padded[:, cols_here : cols_here + window], following, precision=lax.Precision.HIGHEST
    )
    matrix = jnp.concatenate([leading, middle, trailing], axis=1)
    rotations = lax.all_gather(left_off, "col", axis=1, tiled=True)
    following = passed_along(rotations[0][:, :half_window], "row", -1)
    padded = padded_2(matrix, (("row", 0),), half_window)
    leading = jnp.dot(
        rotations[0][:, half_window:].T, padded[:window], precision=lax.Precision.HIGHEST
    )
    middle = apply_left(padded[window:rows_here], rotations[1:])
    trailing = jnp.dot(
        following.T, padded[rows_here : rows_here + window], precision=lax.Precision.HIGHEST
    )
    return jnp.concatenate([leading, middle, trailing], axis=0)


def solution(mesh):
    return jax.shard_map(
        body,
        mesh=mesh,
        in_specs=(
            P("row", "col"),
            P("row", "col", None),
            P("col", "row", None),
            P("row", "col", None),
            P("col", "row", None),
        ),
        out_specs=P("row", "col"),
        check_vma=False,
    )
```

profile of v0, /device:TPU:1, one launch (start us, length us, event | category | flops | bytes accessed | tf_op | source)
XLA Modules:
  0.0 192.9 jit_solution(4929643086227449214)
XLA Ops:
  6.5 0.0 copy-start
  6.5 0.0 all-gather.5.cloned.1.call-start
  6.5 0.7 all-gather.5.cloned.1.call-update
  7.3 0.0 all-gather.7.cloned.1.call-start
  7.3 0.7 all-gather.7.cloned.1.call-update
  8.0 0.0 all-gather.9.cloned.1.call-start
  8.1 0.7 all-gather.9.cloned.1.call-update
  8.7 0.0 all-gather.11.cloned.1.call-start
  8.8 0.5 all-gather.11.cloned.1.call-update
  9.3 18.8 %all-gather.5.cloned.1.call-done = f32[1,512,512]{2,1,0:T(8,128)} async-done(((f32[1,128,512]{2,1,0:T(8,128)}), f32[1,512,512]{2,1,0:T(8,128)}) %all-gather.5.cloned.1.call-update) | async-done | bytes 1048592 | tf_op jit(solution)/shard_map/all_gather | solution.py:49
  28.1 0.0 copy-done
  28.1 9.3 %convolution_bitcast_fusion = f32[1024,1,512]{0,2,1:T(8,128)} fusion(f32[1024,512]{1,0:T(8,128)S(1)} %copy-done, f32[1,512,512]{2,1,0:T(8,128)} %all-gather.5.cloned.1.call-done), kind=kOutput, calls=%fused_computation.9 | convolution fusion | flops 3221225472 | bytes 5242880 | tf_op jit(solution)/shard_map/rka,kab->rkb/dot_general | solution.py:40
  37.3 3.0 %copy.7 = f32[1024,1,512]{2,0,1:T(8,128)} copy(f32[1024,1,512]{0,2,1:T(8,128)} %convolution_bitcast_fusion) | data formatting | bytes 4194304 | tf_op jit(solution)/shard_map/reshape;reshape | solution.py:31
  40.3 36.8 %all-gather.7.cloned.1.call-done = f32[2,512,512]{2,1,0:T(8,128)} async-done(((f32[2,64,512]{2,1,0:T(8,128)}), f32[2,512,512]{2,1,0:T(8,128)}) %all-gather.7.cloned.1.call-update) | async-done | bytes 2097168 | tf_op jit(solution)/shard_map/all_gather | solution.py:51
  77.1 5.8 %fusion.17 = f32[2,512,512]{1,2,0:T(8,128)S(1)} fusion(f32[2,512,512]{2,1,0:T(8,128)} %bitcast.31, f32[2,512,512]{2,1,0:T(8,128)} %all-gather.7.cloned.1.call-done), kind=kOutput, calls=%fused_computation.33 | convolution fusion | flops 3221225472 | bytes 6291456 | tf_op jit(solution)/shard_map/kab,kac->kbc/dot_general | solution.py:32
  82.8 0.0 copy-start.1
  82.8 1.4 fusion.16
  84.2 0.3 copy-done.1
  84.5 0.3 collective-permute-start
  84.8 3.9 %collective-permute-start.1 = (f32[1024,256]{1,0:T(8,128)}, f32[1024,256]{1,0:T(8,128)}, u32[]{:S(2)}, u32[]{:S(2)}) collective-permute-start(f32[1024,256]{1,0:T(8,128)} %get-tuple-element.8), channel_id=1, source_target_pairs={{1,0},{2,1},{3,2},{4,3},{5,4},{6,5},{7,6},{0,7},{9,8},{10,9},{11,1... | collective-permute-start | bytes 3145736 | tf_op jit(solution)/shard_map/ppermute | solution.py:21
  88.7 7.5 %all-gather.9.cloned.1.call-done = f32[1,512,512]{2,1,0:T(8,128)} async-done(((f32[1,128,512]{2,1,0:T(8,128)}), f32[1,512,512]{2,1,0:T(8,128)}) %all-gather.9.cloned.1.call-update) | async-done | bytes 1048592 | tf_op jit(solution)/shard_map/all_gather | solution.py:53
  96.2 1.1 slice.68
  97.3 0.0 copy-start.2
  97.3 4.2 %collective-permute-start.2 = (f32[512,256]{1,0:T(8,128)S(1)}, f32[512,256]{1,0:T(8,128)S(1)}, u32[]{:S(2)}, u32[]{:S(2)}) collective-permute-start(f32[512,256]{1,0:T(8,128)S(1)} %slice.68), channel_id=1, source_target_pairs={{0,7},{1,0},{2,1},{3,2},{4,3},{5,4},{6,5},{7,6},{8,15},{9,8},{10,9... | collective-permute-start | bytes 1572872 | tf_op jit(solution)/shard_map/ppermute | solution.py:9
  101.5 42.8 %collective-permute-done = f32[1024,256]{1,0:T(8,128)} collective-permute-done((f32[1024,256]{1,0:T(8,128)S(1)}, f32[1024,256]{1,0:T(8,128)}, u32[]{:S(2)}, u32[]{:S(2)}) %collective-permute-start) | collective-permute-done | bytes 1048608 | tf_op jit(solution)/shard_map/ppermute | solution.py:19
  144.3 3.6 %fusion.2 = f32[1024,256]{0,1:T(8,128)S(1)} fusion(f32[1024,512]{1,0:T(8,128)} %bitcast.29, f32[1024,256]{1,0:T(8,128)} %collective-permute-done, f32[512,512]{1,0:T(8,128)} %bitcast.33), kind=kOutput, calls=%fused_computation.4 | convolution fusion | flops 1611137024 | bytes 4718592 | tf_op jit(solution)/shard_map/dot_general | solution.py:56
  147.9 6.7 %collective-permute-done.2 = f32[512,256]{1,0:T(8,128)S(1)} collective-permute-done((f32[512,256]{1,0:T(8,128)S(1)}, f32[512,256]{1,0:T(8,128)S(1)}, u32[]{:S(2)}, u32[]{:S(2)}) %collective-permute-start.2) | collective-permute-done | bytes 524320 | tf_op jit(solution)/shard_map/ppermute | solution.py:9
  154.6 0.0 collective-permute-done.1
  154.6 0.0 copy-done.2
  154.6 3.3 %fusion = f32[1024,256]{0,1:T(8,128)S(1)} fusion(f32[512,256]{1,0:T(8,128)S(1)} %collective-permute-done.2, f32[1024,256]{1,0:T(8,128)} %collective-permute-done.1, f32[1024,512]{1,0:T(8,128)S(1)} %bitcast.30), kind=kOutput, calls=%fused_computation.1 | convolution fusion | flops 1611137024 | bytes 4718592 | tf_op jit(solution)/shard_map/dot_general | solution.py:60
  157.9 0.0 copy-start.3
  157.9 1.0 copy-done.3
  158.9 1.0 pad_maximum_fusion.14
  159.9 3.7 %collective-permute-start.3 = (f32[256,512]{0,1:T(8,128)}, f32[256,512]{0,1:T(8,128)}, u32[]{:S(2)}, u32[]{:S(2)}) collective-permute-start(f32[256,512]{0,1:T(8,128)} %get-tuple-element.5), channel_id=1, source_target_pairs={{0,8},{8,16},{16,24},{24,0},{1,9},{9,17},{17,25},{25,1},{2,10},{10... | collective-permute-start | bytes 1572872 | tf_op jit(solution)/shard_map/ppermute | solution.py:19
  163.6 4.1 %all-gather.11.cloned.1.call-done = f32[2,512,512]{2,1,0:T(8,128)} async-done(((f32[2,64,512]{2,1,0:T(8,128)}), f32[2,512,512]{2,1,0:T(8,128)}) %all-gather.11.cloned.1.call-update) | async-done | bytes 2097168 | tf_op jit(solution)/shard_map/all_gather | solution.py:64
  167.7 0.0 copy-start.4
  167.7 1.4 slice_bitcast_fusion.2
  169.2 1.0 collective-permute-start.5
  170.2 0.6 collective-permute-start.4
  170.8 0.0 copy-done.4
  170.8 0.0 copy-done.5
  170.9 1.9 convolution_bitcast_fusion.1
  172.7 0.0 collective-permute-done.3
  172.7 2.1 %convolution_bitcast_fusion.3 = f32[256,512]{1,0:T(8,128)S(1)} fusion(f32[256,512]{0,1:T(8,128)} %collective-permute-done.3, f32[1024,256]{0,1:T(8,128)S(1)} %copy-done.4, f32[1024,256]{0,1:T(8,128)S(1)} %fusion.2, f32[512,512]{1,0:T(8,128)S(1)} %slice_bitcast_fusion.2), kind=kOutput, calls=%fused_computation.12 | convolution fusion | flops 805830656 | bytes 3670016 | tf_op jit(solution)/shard_map/dot_general | solution.py:67
  174.9 3.3 %collective-permute-done.5 = f32[512,256]{1,0:T(8,128)S(1)} collective-permute-done((f32[512,256]{1,0:T(8,128)S(1)}, f32[512,256]{1,0:T(8,128)S(1)}, u32[]{:S(2)}, u32[]{:S(2)}) %collective-permute-start.5) | collective-permute-done | bytes 524320 | tf_op jit(solution)/shard_map/ppermute | solution.py:9
  178.2 5.6 %collective-permute-done.4 = f32[256,512]{0,1:T(8,128)S(1)} collective-permute-done((f32[256,512]{0,1:T(8,128)}, f32[256,512]{0,1:T(8,128)S(1)}, u32[]{:S(2)}, u32[]{:S(2)}) %collective-permute-start.4) | collective-permute-done | bytes 524320 | tf_op jit(solution)/shard_map/ppermute | solution.py:21
  183.8 1.1 convolution_bitcast_fusion.2
  184.9 1.5 pad_maximum_fusion.4
  (2 shorter events, 0.0 us)
Async XLA Ops:
  6.5 21.5 %copy-start = (f32[1024,512]{1,0:T(8,128)S(1)}, f32[1024,512]{1,0:T(8,128)}, u32[]{:S(2)}) copy-start(f32[1024,512]{1,0:T(8,128)} %param.5) | copy-start | bytes 6291460
  6.5 21.5 %all-gather.5.cloned.1.call-start = ((), (), s32[]{:S(2)}) async-start(), calls=%async_computation | async-start | bytes 1310720 | tf_op jit(solution)/shard_map/all_gather | solution.py:49
  7.3 69.8 %all-gather.7.cloned.1.call-start = ((), (), s32[]{:S(2)}) async-start(), calls=%async_computation.1 | async-start | bytes 2359296 | tf_op jit(solution)/shard_map/all_gather | solution.py:51
  8.0 88.2 %all-gather.9.cloned.1.call-start = ((), (), s32[]{:S(2)}) async-start(), calls=%async_computation.2 | async-start | bytes 1310720 | tf_op jit(solution)/shard_map/all_gather | solution.py:53
  8.7 159.0 %all-gather.11.cloned.1.call-start = ((), (), s32[]{:S(2)}) async-start(), calls=%async_computation.3 | async-start | bytes 2359296 | tf_op jit(solution)/shard_map/all_gather | solution.py:64
  82.8 1.7 copy-start.1
  84.5 59.8 %collective-permute-start = (f32[1024,256]{1,0:T(8,128)S(1)}, f32[1024,256]{1,0:T(8,128)}, u32[]{:S(2)}, u32[]{:S(2)}) collective-permute-start(f32[1024,256]{1,0:T(8,128)S(1)} %get-tuple-element.7), channel_id=1, source_target_pairs={{0,1},{1,2},{2,3},{3,4},{4,5},{5,6},{6,7},{7,0},{8,9},{9,10},{10,1... | collective-permute-start | bytes 3145736 | tf_op jit(solution)/shard_map/ppermute | solution.py:19
  84.8 69.9 %collective-permute-start.1 = (f32[1024,256]{1,0:T(8,128)}, f32[1024,256]{1,0:T(8,128)}, u32[]{:S(2)}, u32[]{:S(2)}) collective-permute-start(f32[1024,256]{1,0:T(8,128)} %get-tuple-element.8), channel_id=1, source_target_pairs={{1,0},{2,1},{3,2},{4,3},{5,4},{6,5},{7,6},{0,7},{9,8},{10,9},{11,1... | collective-permute-start | bytes 3145736 | tf_op jit(solution)/shard_map/ppermute | solution.py:21
  97.3 57.4 %copy-start.2 = (f32[2,512,512]{1,2,0:T(8,128)S(1)}, f32[2,512,512]{1,2,0:T(8,128)}, u32[]{:S(2)}) copy-start(f32[2,512,512]{1,2,0:T(8,128)} %copy-done.1) | copy-start | bytes 6291460
  97.3 57.3 %collective-permute-start.2 = (f32[512,256]{1,0:T(8,128)S(1)}, f32[512,256]{1,0:T(8,128)S(1)}, u32[]{:S(2)}, u32[]{:S(2)}) collective-permute-start(f32[512,256]{1,0:T(8,128)S(1)} %slice.68), channel_id=1, source_target_pairs={{0,7},{1,0},{2,1},{3,2},{4,3},{5,4},{6,5},{7,6},{8,15},{9,8},{10,9... | collective-permute-start | bytes 1572872 | tf_op jit(solution)/shard_map/ppermute | solution.py:9
  157.9 1.0 copy-start.3
  159.9 12.8 %collective-permute-start.3 = (f32[256,512]{0,1:T(8,128)}, f32[256,512]{0,1:T(8,128)}, u32[]{:S(2)}, u32[]{:S(2)}) collective-permute-start(f32[256,512]{0,1:T(8,128)} %get-tuple-element.5), channel_id=1, source_target_pairs={{0,8},{8,16},{16,24},{24,0},{1,9},{9,17},{17,25},{25,1},{2,10},{10... | collective-permute-start | bytes 1572872 | tf_op jit(solution)/shard_map/ppermute | solution.py:19
  167.7 3.1 %copy-start.4 = (f32[1024,256]{0,1:T(8,128)S(1)}, f32[1024,256]{0,1:T(8,128)}, u32[]{:S(2)}) copy-start(f32[1024,256]{0,1:T(8,128)} %copy-done.3) | copy-start | bytes 3145732
  167.7 3.1 %copy-start.5 = (f32[2,512,512]{2,1,0:T(8,128)S(1)}, f32[2,512,512]{2,1,0:T(8,128)}, u32[]{:S(2)}) copy-start(f32[2,512,512]{2,1,0:T(8,128)} %all-gather.11.cloned.1.call-done) | copy-start | bytes 6291460
  169.2 9.0 %collective-permute-start.5 = (f32[512,256]{1,0:T(8,128)S(1)}, f32[512,256]{1,0:T(8,128)S(1)}, u32[]{:S(2)}, u32[]{:S(2)}) collective-permute-start(f32[512,256]{1,0:T(8,128)S(1)} %slice.74), channel_id=1, source_target_pairs={{0,24},{8,0},{16,8},{24,16},{1,25},{9,1},{17,9},{25,17},{2,26},{10... | collective-permute-start | bytes 1572872 | tf_op jit(solution)/shard_map/ppermute | solution.py:9
  170.2 13.6 %collective-permute-start.4 = (f32[256,512]{0,1:T(8,128)}, f32[256,512]{0,1:T(8,128)S(1)}, u32[]{:S(2)}, u32[]{:S(2)}) collective-permute-start(f32[256,512]{0,1:T(8,128)} %get-tuple-element.6), channel_id=1, source_target_pairs={{8,0},{16,8},{24,16},{0,24},{9,1},{17,9},{25,17},{1,25},{10,2},{18... | collective-permute-start | bytes 1572872 | tf_op jit(solution)/shard_map/ppermute | solution.py:21
Sparse Core Ops, SparseCore 0:
  8.9 19.1 all-gather.4
  30.3 46.7 all-gather.6
  78.6 17.5 all-gather.8
  98.2 69.4 all-gather.10
where the time goes:
time: 193 us
  waiting for transfers between devices  128 us (66%)
  matrix products  27.1 us (14%)
  starting transfers between devices  13.8 us (7%)
  between operations  13.2 us (7%)
  local copies, waits for them, and re-layouts  8.15 us (4%)
  other arithmetic  2.53 us (1%)
    ppermute x2, waiting for transfers between devices, padded_2(): lax.ppermute(tail, axis, [(i, (i + 1) % count) for i in range(count)])  42.8 us
    all_gather x1, waiting for transfers between devices, body(): rotations = lax.all_gather(left_rot, 'col', axis=1, tiled=True)  36.8 us
    all_gather x1, waiting for transfers between devices, body(): rotations = lax.all_gather(right_rot, 'row', axis=1, tiled=True)  18.8 us
    ppermute x2, waiting for transfers between devices, passed_along(): return lax.ppermute(x, axis, [(i, (i + by) % size) for i in range(size)])  9.97 us
    dot_general x1, matrix products, apply_right(): jnp.einsum('rka,kab->rkb', shaped, rotations, precision=lax.Precision.HIG...  9.25 us
    dot_general x2, matrix products, apply_left(): jnp.einsum('kab,kac->kbc', rotations, shaped, precision=lax.Precision.HIG...  7.62 us
    all_gather x1, waiting for transfers between devices, body(): rotations = lax.all_gather(right_off, 'row', axis=1, tiled=True)  7.54 us
    ppermute x2, waiting for transfers between devices, padded_2(): lax.ppermute(head, axis, [((i + 1) % count, i) for i in range(count)])  5.62 us
  transfers between devices with their start and end apart: 10, of which 8 were waited for; matrix products, arithmetic and copies ran while one was open for 18% of the time, Pallas kernels for 0%

commit v1 on v0

--- a/solution.py
+++ b/solution.py
@@ -46,7 +46,8 @@
     half_window = window // 2
     rows_here = schur.shape[0]
     cols_here = schur.shape[1]
-    rotations = lax.all_gather(right_rot, "row", axis=1, tiled=True)
+    sent = jnp.stack([right_rot] * lax.axis_size("row"))
+    rotations = jnp.concatenate(lax.all_to_all(sent, "row", 0, 0), axis=1)
     matrix = apply_right(schur, rotations)
     rotations = lax.all_gather(left_rot, "col", axis=1, tiled=True)
     matrix = apply_left(matrix, rotations)

time: 193 us -> 175 us (0.907)
  waiting for transfers between devices: 128 us -> 92.5 us
  blocking collectives: 0 us -> 17.4 us
    all_gather x1 -> x0, waiting for transfers between devices: 18.8 us -> none  [body(): rotations = lax.all_gather(right_rot, 'row', axis=1, tiled=True)]
    all_to_all x0 -> x1, blocking collectives: none -> 17.4 us  [body(): rotations = jnp.concatenate(lax.all_to_all(sent, 'row', 0, 0), axis=1)]
    all_gather x1, waiting for transfers between devices: 36.8 us -> 20.4 us  [body(): rotations = lax.all_gather(left_rot, 'col', axis=1, tiled=True)]
  transfers between devices with their start and end apart: 10 -> 9, of which waited for: 8 -> 7; matrix products, arithmetic and copies ran while one was open for 18% -> 19% of each run, Pallas kernels for 0% -> 0%
where the time goes in v1:
time: 175 us
  waiting for transfers between devices  92.5 us (53%)
  matrix products  26 us (15%)
  blocking collectives  17.4 us (10%)
  starting transfers between devices  13.8 us (8%)
  between operations  13.2 us (8%)
  local copies, waits for them, and re-layouts  9.17 us (5%)
  other arithmetic  2.53 us (1%)
    ppermute x2, waiting for transfers between devices, padded_2(): lax.ppermute(tail, axis, [(i, (i + 1) % count) for i in range(count)])  42.8 us
    all_gather x1, waiting for transfers between devices, body(): rotations = lax.all_gather(left_rot, 'col', axis=1, tiled=True)  20.4 us
    all_to_all x1, blocking collectives, body(): rotations = jnp.concatenate(lax.all_to_all(sent, 'row', 0, 0), axis=1)  17.4 us
    ppermute x2, waiting for transfers between devices, passed_along(): return lax.ppermute(x, axis, [(i, (i + by) % size) for i in range(size)])  9.99 us
    dot_general x1, matrix products, apply_right(): jnp.einsum('rka,kab->rkb', shaped, rotations, precision=lax.Precision.HIG...  8.21 us
    dot_general x2, matrix products, apply_left(): jnp.einsum('kab,kac->kbc', rotations, shaped, precision=lax.Precision.HIG...  7.62 us
    all_gather x1, waiting for transfers between devices, body(): rotations = lax.all_gather(right_off, 'row', axis=1, tiled=True)  7.54 us
    ppermute x2, waiting for transfers between devices, padded_2(): lax.ppermute(head, axis, [((i + 1) % count, i) for i in range(count)])  5.62 us
  transfers between devices with their start and end apart: 9, of which 7 were waited for; matrix products, arithmetic and copies ran while one was open for 19% of the time, Pallas kernels for 0%

profile of v1, /device:TPU:1, one launch (start us, length us, event | category | flops | bytes accessed | tf_op | source)
XLA Modules:
  0.0 174.6 jit_solution(11007314293581148346)
XLA Ops:
  6.5 0.0 copy-start
  6.5 0.0 all-gather.4.cloned.1.call-start
  6.5 0.7 all-gather.4.cloned.1.call-update
  7.3 0.0 all-gather.6.cloned.1.call-start
  7.3 0.7 all-gather.6.cloned.1.call-update
  8.0 0.0 all-gather.8.cloned.1.call-start
  8.1 0.7 all-gather.8.cloned.1.call-update
  8.7 1.1 stack.2
  9.8 17.4 %all_to_all.5 = f32[4,1,128,512]{3,2,1,0:T(8,128)S(1)} all-to-all(f32[4,1,128,512]{3,2,1,0:T(8,128)S(1)} %stack.2), channel_id=1, replica_groups=mesh['row'=4,'col'=8] {'row'}, dimensions={0} | all-to-all | bytes 2097152 | tf_op jit(solution)/shard_map/all_to_all | solution.py:50
  27.3 0.0 copy-done
  27.3 8.2 %convolution_bitcast_fusion = f32[1024,1,512]{0,2,1:T(8,128)} fusion(f32[512,512]{1,0:T(8,128)S(1)} %bitcast.32, f32[1024,512]{1,0:T(8,128)S(1)} %copy-done), kind=kOutput, calls=%fused_computation.9 | convolution fusion | flops 3221225472 | bytes 5242880 | tf_op jit(solution)/shard_map/rka,kab->rkb/dot_general | solution.py:40
  35.5 2.9 %copy.7 = f32[1024,1,512]{2,0,1:T(8,128)} copy(f32[1024,1,512]{0,2,1:T(8,128)} %convolution_bitcast_fusion) | data formatting | bytes 4194304 | tf_op jit(solution)/shard_map/reshape;reshape | solution.py:31
  38.4 20.4 %all-gather.4.cloned.1.call-done = f32[2,512,512]{2,1,0:T(8,128)} async-done(((f32[2,64,512]{2,1,0:T(8,128)}), f32[2,512,512]{2,1,0:T(8,128)}) %all-gather.4.cloned.1.call-update) | async-done | bytes 2097168 | tf_op jit(solution)/shard_map/all_gather | solution.py:52
  58.8 5.8 %fusion.16 = f32[2,512,512]{1,2,0:T(8,128)S(1)} fusion(f32[2,512,512]{2,1,0:T(8,128)} %bitcast.31, f32[2,512,512]{2,1,0:T(8,128)} %all-gather.4.cloned.1.call-done), kind=kOutput, calls=%fused_computation.32 | convolution fusion | flops 3221225472 | bytes 6291456 | tf_op jit(solution)/shard_map/kab,kac->kbc/dot_general | solution.py:32
  64.5 0.0 copy-start.1
  64.5 1.3 fusion.15
  65.9 0.3 copy-done.1
  66.2 0.3 collective-permute-start
  66.5 3.9 %collective-permute-start.1 = (f32[1024,256]{1,0:T(8,128)}, f32[1024,256]{1,0:T(8,128)}, u32[]{:S(2)}, u32[]{:S(2)}) collective-permute-start(f32[1024,256]{1,0:T(8,128)} %get-tuple-element.8), channel_id=1, source_target_pairs={{1,0},{2,1},{3,2},{4,3},{5,4},{6,5},{7,6},{0,7},{9,8},{10,9},{11,1... | collective-permute-start | bytes 3145736 | tf_op jit(solution)/shard_map/ppermute | solution.py:21
  70.4 7.5 %all-gather.6.cloned.1.call-done = f32[1,512,512]{2,1,0:T(8,128)} async-done(((f32[1,128,512]{2,1,0:T(8,128)}), f32[1,512,512]{2,1,0:T(8,128)}) %all-gather.6.cloned.1.call-update) | async-done | bytes 1048592 | tf_op jit(solution)/shard_map/all_gather | solution.py:54
  77.9 1.1 slice.68
  79.0 0.0 copy-start.2
  79.0 4.2 %collective-permute-start.2 = (f32[512,256]{1,0:T(8,128)S(1)}, f32[512,256]{1,0:T(8,128)S(1)}, u32[]{:S(2)}, u32[]{:S(2)}) collective-permute-start(f32[512,256]{1,0:T(8,128)S(1)} %slice.68), channel_id=1, source_target_pairs={{0,7},{1,0},{2,1},{3,2},{4,3},{5,4},{6,5},{7,6},{8,15},{9,8},{10,9... | collective-permute-start | bytes 1572872 | tf_op jit(solution)/shard_map/ppermute | solution.py:9
  83.2 42.8 %collective-permute-done = f32[1024,256]{1,0:T(8,128)} collective-permute-done((f32[1024,256]{1,0:T(8,128)S(1)}, f32[1024,256]{1,0:T(8,128)}, u32[]{:S(2)}, u32[]{:S(2)}) %collective-permute-start) | collective-permute-done | bytes 1048608 | tf_op jit(solution)/shard_map/ppermute | solution.py:19
  126.0 3.6 %fusion.2 = f32[1024,256]{0,1:T(8,128)S(1)} fusion(f32[1024,512]{1,0:T(8,128)} %bitcast.29, f32[1024,256]{1,0:T(8,128)} %collective-permute-done, f32[512,512]{1,0:T(8,128)} %bitcast.34), kind=kOutput, calls=%fused_computation.4 | convolution fusion | flops 1611137024 | bytes 4718592 | tf_op jit(solution)/shard_map/dot_general | solution.py:57
  129.6 6.7 %collective-permute-done.2 = f32[512,256]{1,0:T(8,128)S(1)} collective-permute-done((f32[512,256]{1,0:T(8,128)S(1)}, f32[512,256]{1,0:T(8,128)S(1)}, u32[]{:S(2)}, u32[]{:S(2)}) %collective-permute-start.2) | collective-permute-done | bytes 524320 | tf_op jit(solution)/shard_map/ppermute | solution.py:9
  136.3 0.0 collective-permute-done.1
  136.3 0.0 copy-done.2
  136.3 3.3 %fusion = f32[1024,256]{0,1:T(8,128)S(1)} fusion(f32[512,256]{1,0:T(8,128)S(1)} %collective-permute-done.2, f32[1024,256]{1,0:T(8,128)} %collective-permute-done.1, f32[1024,512]{1,0:T(8,128)S(1)} %bitcast.30), kind=kOutput, calls=%fused_computation.1 | convolution fusion | flops 1611137024 | bytes 4718592 | tf_op jit(solution)/shard_map/dot_general | solution.py:61
  139.6 0.0 copy-start.3
  139.6 1.0 copy-done.3
  140.6 1.0 pad_maximum_fusion.14
  141.6 3.7 %collective-permute-start.3 = (f32[256,512]{0,1:T(8,128)}, f32[256,512]{0,1:T(8,128)}, u32[]{:S(2)}, u32[]{:S(2)}) collective-permute-start(f32[256,512]{0,1:T(8,128)} %get-tuple-element.5), channel_id=1, source_target_pairs={{0,8},{8,16},{16,24},{24,0},{1,9},{9,17},{17,25},{25,1},{2,10},{10... | collective-permute-start | bytes 1572872 | tf_op jit(solution)/shard_map/ppermute | solution.py:19
  145.4 4.1 %all-gather.8.cloned.1.call-done = f32[2,512,512]{2,1,0:T(8,128)} async-done(((f32[2,64,512]{2,1,0:T(8,128)}), f32[2,512,512]{2,1,0:T(8,128)}) %all-gather.8.cloned.1.call-update) | async-done | bytes 2097168 | tf_op jit(solution)/shard_map/all_gather | solution.py:65
  149.4 0.0 copy-start.4
  149.4 0.0 copy-start.5
  149.4 1.4 slice_bitcast_fusion.2
  150.9 1.0 collective-permute-start.5
  151.9 0.6 collective-permute-start.4
  152.6 0.0 copy-done.4
  152.6 0.0 copy-done.5
  152.6 1.9 %convolution_bitcast_fusion.1 = f32[512,512]{1,0:T(8,128)S(1)} fusion(f32[1024,256]{0,1:T(8,128)S(1)} %fusion.2, f32[1024,256]{0,1:T(8,128)S(1)} %copy-done.4, f32[2,512,512]{2,1,0:T(8,128)S(1)} %copy-done.5), kind=kOutput, calls=%fused_computation.10 | convolution fusion | flops 1610874880 | bytes 4194304 | tf_op jit(solution)/shard_map/kab,kac->kbc/dot_general | solution.py:32
  154.4 0.0 collective-permute-done.3
  154.4 2.1 %convolution_bitcast_fusion.3 = f32[256,512]{1,0:T(8,128)S(1)} fusion(f32[256,512]{0,1:T(8,128)} %collective-permute-done.3, f32[1024,256]{0,1:T(8,128)S(1)} %copy-done.4, f32[1024,256]{0,1:T(8,128)S(1)} %fusion.2, f32[512,512]{1,0:T(8,128)S(1)} %slice_bitcast_fusion.2), kind=kOutput, calls=%fused_computation.12 | convolution fusion | flops 805830656 | bytes 3670016 | tf_op jit(solution)/shard_map/dot_general | solution.py:68
  156.6 3.3 %collective-permute-done.5 = f32[512,256]{1,0:T(8,128)S(1)} collective-permute-done((f32[512,256]{1,0:T(8,128)S(1)}, f32[512,256]{1,0:T(8,128)S(1)}, u32[]{:S(2)}, u32[]{:S(2)}) %collective-permute-start.5) | collective-permute-done | bytes 524320 | tf_op jit(solution)/shard_map/ppermute | solution.py:9
  159.9 5.6 %collective-permute-done.4 = f32[256,512]{0,1:T(8,128)S(1)} collective-permute-done((f32[256,512]{0,1:T(8,128)}, f32[256,512]{0,1:T(8,128)S(1)}, u32[]{:S(2)}, u32[]{:S(2)}) %collective-permute-start.4) | collective-permute-done | bytes 524320 | tf_op jit(solution)/shard_map/ppermute | solution.py:21
  165.5 1.1 convolution_bitcast_fusion.2
  166.6 1.5 pad_maximum_fusion.4
  (1 shorter events, 0.0 us)
Async XLA Ops:
  6.5 20.7 %copy-start = (f32[1024,512]{1,0:T(8,128)S(1)}, f32[1024,512]{1,0:T(8,128)}, u32[]{:S(2)}) copy-start(f32[1024,512]{1,0:T(8,128)} %param.5) | copy-start | bytes 6291460
  6.5 52.2 %all-gather.4.cloned.1.call-start = ((), (), s32[]{:S(2)}) async-start(), calls=%async_computation.1 | async-start | bytes 2359296 | tf_op jit(solution)/shard_map/all_gather | solution.py:52
  7.3 70.6 %all-gather.6.cloned.1.call-start = ((), (), s32[]{:S(2)}) async-start(), calls=%async_computation.2 | async-start | bytes 1310720 | tf_op jit(solution)/shard_map/all_gather | solution.py:54
  8.0 141.4 %all-gather.8.cloned.1.call-start = ((), (), s32[]{:S(2)}) async-start(), calls=%async_computation.3 | async-start | bytes 2359296 | tf_op jit(solution)/shard_map/all_gather | solution.py:65
  64.5 1.7 copy-start.1
  66.2 59.8 %collective-permute-start = (f32[1024,256]{1,0:T(8,128)S(1)}, f32[1024,256]{1,0:T(8,128)}, u32[]{:S(2)}, u32[]{:S(2)}) collective-permute-start(f32[1024,256]{1,0:T(8,128)S(1)} %get-tuple-element.7), channel_id=1, source_target_pairs={{0,1},{1,2},{2,3},{3,4},{4,5},{5,6},{6,7},{7,0},{8,9},{9,10},{10,1... | collective-permute-start | bytes 3145736 | tf_op jit(solution)/shard_map/ppermute | solution.py:19
  66.5 69.9 %collective-permute-start.1 = (f32[1024,256]{1,0:T(8,128)}, f32[1024,256]{1,0:T(8,128)}, u32[]{:S(2)}, u32[]{:S(2)}) collective-permute-start(f32[1024,256]{1,0:T(8,128)} %get-tuple-element.8), channel_id=1, source_target_pairs={{1,0},{2,1},{3,2},{4,3},{5,4},{6,5},{7,6},{0,7},{9,8},{10,9},{11,1... | collective-permute-start | bytes 3145736 | tf_op jit(solution)/shard_map/ppermute | solution.py:21
  79.0 57.4 %copy-start.2 = (f32[2,512,512]{1,2,0:T(8,128)S(1)}, f32[2,512,512]{1,2,0:T(8,128)}, u32[]{:S(2)}) copy-start(f32[2,512,512]{1,2,0:T(8,128)} %copy-done.1) | copy-start | bytes 6291460
  79.0 57.3 %collective-permute-start.2 = (f32[512,256]{1,0:T(8,128)S(1)}, f32[512,256]{1,0:T(8,128)S(1)}, u32[]{:S(2)}, u32[]{:S(2)}) collective-permute-start(f32[512,256]{1,0:T(8,128)S(1)} %slice.68), channel_id=1, source_target_pairs={{0,7},{1,0},{2,1},{3,2},{4,3},{5,4},{6,5},{7,6},{8,15},{9,8},{10,9... | collective-permute-start | bytes 1572872 | tf_op jit(solution)/shard_map/ppermute | solution.py:9
  139.6 1.0 copy-start.3
  141.6 12.8 %collective-permute-start.3 = (f32[256,512]{0,1:T(8,128)}, f32[256,512]{0,1:T(8,128)}, u32[]{:S(2)}, u32[]{:S(2)}) collective-permute-start(f32[256,512]{0,1:T(8,128)} %get-tuple-element.5), channel_id=1, source_target_pairs={{0,8},{8,16},{16,24},{24,0},{1,9},{9,17},{17,25},{25,1},{2,10},{10... | collective-permute-start | bytes 1572872 | tf_op jit(solution)/shard_map/ppermute | solution.py:19
  149.4 3.1 %copy-start.4 = (f32[1024,256]{0,1:T(8,128)S(1)}, f32[1024,256]{0,1:T(8,128)}, u32[]{:S(2)}) copy-start(f32[1024,256]{0,1:T(8,128)} %copy-done.3) | copy-start | bytes 3145732
  149.4 3.1 %copy-start.5 = (f32[2,512,512]{2,1,0:T(8,128)S(1)}, f32[2,512,512]{2,1,0:T(8,128)}, u32[]{:S(2)}) copy-start(f32[2,512,512]{2,1,0:T(8,128)} %all-gather.8.cloned.1.call-done) | copy-start | bytes 6291460
  150.9 9.0 %collective-permute-start.5 = (f32[512,256]{1,0:T(8,128)S(1)}, f32[512,256]{1,0:T(8,128)S(1)}, u32[]{:S(2)}, u32[]{:S(2)}) collective-permute-start(f32[512,256]{1,0:T(8,128)S(1)} %slice.74), channel_id=1, source_target_pairs={{0,24},{8,0},{16,8},{24,16},{1,25},{9,1},{17,9},{25,17},{2,26},{10... | collective-permute-start | bytes 1572872 | tf_op jit(solution)/shard_map/ppermute | solution.py:9
  151.9 13.6 %collective-permute-start.4 = (f32[256,512]{0,1:T(8,128)}, f32[256,512]{0,1:T(8,128)S(1)}, u32[]{:S(2)}, u32[]{:S(2)}) collective-permute-start(f32[256,512]{0,1:T(8,128)} %get-tuple-element.6), channel_id=1, source_target_pairs={{8,0},{16,8},{24,16},{0,24},{9,1},{17,9},{25,17},{1,25},{10,2},{18... | collective-permute-start | bytes 1572872 | tf_op jit(solution)/shard_map/ppermute | solution.py:21
Sparse Core Ops, SparseCore 0:
  9.5 49.2 all-gather.3
  60.3 17.5 all-gather.5
  80.1 69.2 all-gather.7
